TPU v7x, 32 devices: a whole 2x2x4 slice. The times are simulated.
32 devices in a mesh: dp: 8 (over z, x), tensor: 4 (over y, core).
Axes of the slice: x: 2, y: 2, z: 4, core: 2. Of those that a mesh axis runs over, the one named last changes fastest.
Arguments:
- query_states: bfloat16 [1, 8192, 1024], P(None, 'dp', 'tensor'), may hold values from -6 to 6
- key_states: bfloat16 [1, 8192, 1024], P(None, 'dp', 'tensor'), may hold values from -6 to 6
- value_states: bfloat16 [1, 8192, 1024], P(None, 'dp', 'tensor'), may hold values from -6 to 6
- joining_weight: bfloat16 [1, 1024, 2048], P(None, 'tensor'), may hold values from -0.1875 to 0.1875
- norm_gain: float32 [2048], replicated, may hold values from 0.1 to 1.9
- next_hidden: bfloat16 [8192, 2048], P(('dp', 'tensor')), may hold values from -6 to 6
- lengths: int32 [8], P('dp'), may hold values from 256 to 1024
- vote_counts: int32 [8], P('dp'), may hold values from 1 to 8
Outputs:
- draft_hidden: bfloat16 [8192, 2048], P(('dp', 'tensor'))
- weight_grad: bfloat16 [1, 1024, 2048], P(None, 'tensor', 'dp')
- gain_grad: float32 [2048], replicated
- draft_loss: float32 [], replicated
All inputs are finite; a program needn't handle non-finite values.
Results may differ from a plain program's by a relative error of at most 0.014.
Values may be sent and summed in bfloat16 or wider, within the bound.
No kernel may reach another device: no remote copies, remote signals or barrier semaphores. Data moves between devices by JAX's collectives and lax.ppermute only.
A program may use at most 64 MiB of HBM per device.

v0:
```python
import math
import jax
import jax.numpy as jnp
from jax import lax
from jax.sharding import PartitionSpec as P

HD = 128
loss_scale = 65536.0
neg_large = -1e30


def on_device(
    query_states,
    key_states,
    value_states,
    joining_weight,
    norm_gain,
    next_hidden,
    lengths,
    vote_counts,
):
    n_layers, tok_group, col_width = query_states.shape
    chains = lengths.shape[0]
    seq_len = tok_group // chains
    heads_here = col_width // HD
    shaped = (n_layers, chains, seq_len, heads_here, HD)
    scores = jnp.einsum(
        "lcqhd,lckhd->lchqk",
        query_states.reshape(shaped),
        key_states.reshape(shaped),
        preferred_element_type=jnp.float32,
    ) / math.sqrt(HD)
    positions = jnp.arange(seq_len)
    causal = positions[None, :] <= positions[:, None]
    key_valid = positions[None, :] < lengths[:, None]
    visible = causal[None, None, None, :, :] & key_valid[None, :, None, None, :]
    scores = jnp.where(visible, scores, neg_large)
    row_peak = jnp.max(scores, axis=-1, keepdims=True)
    exponent = jnp.exp(scores - row_peak)
    attn_probs = (exponent / jnp.sum(exponent, axis=-1, keepdims=True)).astype(jnp.bfloat16)
    context = jnp.einsum(
        "lchqk,lckhd->lcqhd",
        attn_probs,
        value_states.reshape(shaped),
        preferred_element_type=jnp.float32,
    )
    context = context.astype(jnp.bfloat16).reshape(n_layers, tok_group, col_width)
    own_rows = next_hidden.shape[0]
    offset = lax.axis_index("tensor") * own_rows
    partial_sum = jnp.einsum(
        "ltc,lcd->td", context, joining_weight, preferred_element_type=jnp.float32
    )
    summed = lax.psum(partial_sum.astype(jnp.bfloat16), "tensor").astype(jnp.float32)
    joined_rows = lax.dynamic_slice_in_dim(summed, offset, own_rows, 0)
    token_pos = offset + jnp.arange(own_rows, dtype=jnp.int32)
    chain_of = token_pos // seq_len
    in_chain = token_pos % seq_len
    onehot = (chain_of[:, None] == jnp.arange(chains)[None, :]).astype(jnp.float32)
    tok_votes = jnp.dot(onehot, vote_counts.astype(jnp.float32), precision=lax.Precision.HIGHEST)
    tok_length = jnp.dot(onehot, lengths.astype(jnp.float32), precision=lax.Precision.HIGHEST)
    token_weight = jnp.where(in_chain.astype(jnp.float32) < tok_length - 1.0, tok_votes, 0.0)
    inv_rms = lax.rsqrt(jnp.mean(joined_rows * joined_rows, axis=-1, keepdims=True) + 1e-06)
    normed = joined_rows * inv_rms
    predicted = normed * norm_gain
    draft_hidden = predicted.astype(jnp.bfloat16)
    misfit = predicted - next_hidden.astype(jnp.float32)
    local_loss = jnp.sum(token_weight * jnp.mean(misfit * misfit, axis=-1))
    grad_pred = loss_scale * 2.0 / joined_rows.shape[1] * token_weight[:, None] * misfit
    local_gain = jnp.sum(grad_pred * normed, axis=0)
    grad_normed = grad_pred * norm_gain
    grad_joined = (
        inv_rms * (grad_normed - normed * jnp.mean(grad_normed * normed, axis=-1, keepdims=True))
    ).astype(jnp.bfloat16)
    gain_sum, loss_sum, weight_total = lax.psum(
        (local_gain, local_loss, jnp.sum(token_weight)), ("dp", "tensor")
    )
    grad_total = jnp.einsum(
        "ltc,td->lcd",
        context,
        lax.all_gather(grad_joined, "tensor", axis=0, tiled=True),
        preferred_element_type=jnp.float32,
    )
    grad_cols = lax.psum_scatter(
        grad_total.astype(jnp.bfloat16), "dp", scatter_dimension=2, tiled=True
    ).astype(jnp.float32)
    weight_grad = (grad_cols / weight_total).astype(jnp.bfloat16)
    return (draft_hidden, weight_grad, gain_sum / weight_total, loss_sum / weight_total)


def solution(mesh):
    return jax.shard_map(
        on_device,
        mesh=mesh,
        in_specs=(
            P(None, "dp", "tensor"),
            P(None, "dp", "tensor"),
            P(None, "dp", "tensor"),
            P(None, "tensor", None),
            P(),
            P(("dp", "tensor"), None),
            P("dp"),
            P("dp"),
        ),
        out_specs=(P(("dp", "tensor"), None), P(None, "tensor", "dp"), P(), P()),
        check_vma=False,
    )
```

profile of v0, /device:TPU:0, one launch (start us, length us, event | category | flops | bytes accessed | tf_op | source)
XLA Modules:
  0.0 236.3 jit_solution(4800602347688197091)
XLA Ops:
  7.2 0.0 all-reduce.3.cloned.1.call-start
  8.0 0.4 fusion.4
  8.4 2.0 reshape.122
  10.4 1.0 reshape.123
  11.4 1.0 copy.17
  12.4 7.7 %fusion.39 = (f32[2,1024]{1,0:T(2,128)S(1)}, f32[2,1024,1024]{1,2,0:T(8,128)}) fusion(pred[1024,1024]{0,1:T(8,128)(4,1)S(1)} %fusion.4, bf16[1024,2,128]{2,1,0:T(2,128)(2,1)} %reshape.123, bf16[1024,2,128]{2,1,0:T(2,128)(2,1)} %reshape.122), kind=kOutput, calls=%fused_computation.54 | convolution fusion | flops 545260544 | bytes 10493952 | tf_op jit(solution)/shard_map/sub | solution.py:39
  20.1 4.1 %fusion.20 = bf16[2,1024,128]{1,2,0:T(8,128)(2,1)S(1)} fusion(bf16[1024,2,128]{0,2,1:T(8,128)(2,1)S(1)} %bitcast.23, f32[2,1024,1024]{1,2,0:T(8,128)} %get-tuple-element.13, f32[2,1024]{1,0:T(2,128)S(1)} %get-tuple-element.12), kind=kOutput, calls=%fused_computation.29 | convolution fusion | flops 541327360 | bytes 9445376 | tf_op jit(solution)/shard_map/lchqk,lckhd->lcqhd/dot_general | solution.py:41
  24.3 3.3 %convolution_convert_fusion = bf16[1024,2048]{1,0:T(8,128)(2,1)} fusion(bf16[1024,256]{0,1:T(8,128)(2,1)S(1)} %bitcast.21, bf16[1,256,2048]{2,1,0:T(8,128)(2,1)S(1)} %copy-done), kind=kOutput, calls=%fused_computation.11 | convolution fusion | flops 1075838976 | bytes 5767168 | tf_op jit(solution)/shard_map/ltc,lcd->td/dot_general | solution.py:50
  27.5 0.0 all-reduce.3.cloned.1.call-update
  27.6 0.0 all-gather.2.cloned.1.call-start
  28.3 0.6 broadcast_multiply_fusion
  29.0 86.9 %all-reduce.3.cloned.1.call-done = bf16[1024,2048]{1,0:T(8,128)(2,1)} async-done(((bf16[1024,2048]{1,0:T(8,128)(2,1)}), bf16[1024,2048]{1,0:T(8,128)(2,1)}) %all-reduce.3.cloned.1.call-update) | async-done | bytes 4194320 | tf_op jit(solution)/shard_map/psum | solution.py:53
  115.9 1.5 fusion.19
  117.4 2.3 fusion.18
  119.8 3.4 %fusion.17 = (bf16[256,2048]{1,0:T(8,128)(2,1)}, bf16[256,2048]{1,0:T(8,128)(2,1)}) fusion(bf16[256,2048]{1,0:T(8,128)(2,1)S(1)} %copy-done.1, f32[256]{0:T(256)S(1)} %broadcast_multiply_fusion.1, f32[256]{0:T(256)S(1)} %get-tuple-element.14, f32[2048]{0:T(1024)S(1)} %copy-done.5, f32[256]{0:T(256)S(1)} %add_rsqrt_fusion, ...), kind=kLoop, calls=%fused_computation.25 | loop fusion | flops 6291456 | bytes 4205572 | tf_op jit(solution)/shard_map/convert_element_type | solution.py:73
  123.2 0.0 all-gather.2.cloned.1.call-update
  123.2 0.0 reduce-scatter.2.cloned.1.call-start
  123.3 34.7 %all-gather.2.cloned.1.call-done = bf16[1024,2048]{1,0:T(8,128)(2,1)} async-done(((bf16[256,2048]{1,0:T(8,128)(2,1)}), bf16[1024,2048]{1,0:T(8,128)(2,1)}) %all-gather.2.cloned.1.call-update) | async-done | bytes 4194320 | tf_op jit(solution)/shard_map/all_gather | solution.py:80
  158.0 4.4 %fusion.11 = bf16[1,256,2048]{2,1,0:T(8,128)(2,1)} fusion(bf16[1024,256]{0,1:T(8,128)(2,1)S(1)} %bitcast.22, bf16[1024,2048]{1,0:T(8,128)(2,1)} %all-gather.2.cloned.1.call-done), kind=kOutput, calls=%fused_computation.19 | convolution fusion | flops 1074266112 | bytes 5767168 | tf_op jit(solution)/shard_map/ltc,td->lcd/dot_general | solution.py:77
  162.4 0.7 multiply_reduce_fusion.1
  163.1 39.7 %all-reduce = (f32[]{:T(128)}, f32[2048]{0:T(1024)S(1)}, f32[]{:T(128)}) all-reduce(f32[]{:T(128)} %get-tuple-element.15, f32[2048]{0:T(1024)S(1)} %get-tuple-element.4, f32[]{:T(128)} %multiply_reduce_fusion.1), channel_id=1, replica_groups=mesh['dp'=8,'tensor'=4] {'dp','tensor'}, use_global_device_ids=true, to_apply=%region_7.8 | all-reduce | flops 2050 | bytes 16400 | tf_op jit(solution)/shard_map/psum | solution.py:74
  204.1 1.2 broadcast_divide_fusion
  205.2 21.3 %reduce-scatter.2.cloned.1.call-done = bf16[1,256,256]{2,1,0:T(8,128)(2,1)} async-done(((bf16[1,256,2048]{2,1,0:T(8,128)(2,1)}), bf16[1,256,256]{2,1,0:T(8,128)(2,1)}) %reduce-scatter.2.cloned.1.call-update) | async-done | bytes 131088 | tf_op jit(solution)/shard_map/reduce_scatter | solution.py:83
  226.5 2.1 divide_convert_fusion.4
  (16 shorter events, 0.1 us)
Async XLA Ops:
  7.2 17.1 %copy-start = (bf16[1,256,2048]{2,1,0:T(8,128)(2,1)S(1)}, bf16[1,256,2048]{2,1,0:T(8,128)(2,1)}, u32[]{:S(2)}) copy-start(bf16[1,256,2048]{2,1,0:T(8,128)(2,1)} %param.11) | copy-start | bytes 3145732
  7.2 3.3 %copy-start.2 = (bf16[1,1024,256]{2,1,0:T(8,128)(2,1)S(1)}, bf16[1,1024,256]{2,1,0:T(8,128)(2,1)}, u32[]{:S(2)}) copy-start(bf16[1,1024,256]{2,1,0:T(8,128)(2,1)} %param.9) | copy-start | bytes 1572868
  7.2 4.2 %copy-start.3 = (bf16[1,1024,256]{2,1,0:T(8,128)(2,1)S(1)}, bf16[1,1024,256]{2,1,0:T(8,128)(2,1)}, u32[]{:S(2)}) copy-start(bf16[1,1024,256]{2,1,0:T(8,128)(2,1)} %param.10) | copy-start | bytes 1572868
  7.2 108.7 %all-reduce.3.cloned.1.call-start = ((), (), s32[]{:S(2)}) async-start(), calls=%async_computation.1 | async-start | bytes 8388608 | tf_op jit(solution)/shard_map/psum | solution.py:53
  12.4 7.7 %copy-start.4 = (bf16[1,1024,256]{1,2,0:T(8,128)(2,1)S(1)}, bf16[1,1024,256]{1,2,0:T(8,128)(2,1)}, u32[]{:S(2)}) copy-start(bf16[1,1024,256]{1,2,0:T(8,128)(2,1)} %copy.17) | copy-start | bytes 1572868
  27.5 89.9 %copy-start.1 = (bf16[256,2048]{1,0:T(8,128)(2,1)S(1)}, bf16[256,2048]{1,0:T(8,128)(2,1)}, u32[]{:S(2)}) copy-start(bf16[256,2048]{1,0:T(8,128)(2,1)} %param.13) | copy-start | bytes 3145732
  27.5 89.9 %copy-start.5 = (f32[2048]{0:T(1024)S(1)}, f32[2048]{0:T(1024)}, u32[]{:S(2)}) copy-start(f32[2048]{0:T(1024)} %param.12) | copy-start | bytes 24580
  27.6 130.4 %all-gather.2.cloned.1.call-start = ((), (), s32[]{:S(2)}) async-start(), calls=%async_computation.2 | async-start | bytes 5242880 | tf_op jit(solution)/shard_map/all_gather | solution.py:80
  123.2 103.3 %reduce-scatter.2.cloned.1.call-start = ((), (), s32[]{:S(2)}) async-start(), calls=%async_computation.3 | async-start | bytes 1179648 | tf_op jit(solution)/shard_map/reduce_scatter | solution.py:83
Sparse Core Ops, SparseCore 0:
  27.7 88.1 all-reduce.2
  123.3 34.6 all-gather.1
  162.5 63.9 reduce-scatter.1
where the time goes:
time: 237 us; the launch traced here: 236 us
  waiting for transfers between devices  143 us (60%)
  blocking collectives  39.7 us (17%)
  matrix products  19.5 us (8%)
  between operations  17.7 us (7%)
  other arithmetic  12.2 us (5%)
  local copies, waits for them, and re-layouts  4.04 us (2%)
    psum x1, waiting for transfers between devices, on_device(): lax.psum(partial_sum.astype(jnp.bfloat16), 'tensor').astype(jnp.float32)  86.9 us
    psum x1, blocking collectives, on_device(): lax.psum((local_gain, local_loss, jnp.sum(token_weight)), ('dp', 'tensor'))  39.7 us
    all_gather x1, waiting for transfers between devices, on_device(): lax.all_gather(grad_joined, 'tensor', axis=0, tiled=True)  34.7 us
    reduce_scatter x1, waiting for transfers between devices, on_device(): lax.psum_scatter(grad_total.astype(jnp.bfloat16), 'dp', scatter_dimension...  21.3 us
    sub x1, matrix products, on_device(): exponent = jnp.exp(scores - row_peak)  7.73 us
  transfers between devices with their start and end apart: 3, of which 3 were waited for; matrix products, arithmetic and copies ran while one was open for 1% of the time, Pallas kernels for 0%

commit v1 on v0

--- a/solution.py
+++ b/solution.py
@@ -7,6 +7,11 @@
 HD = 128
 loss_scale = 65536.0
 neg_large = -1e30
+
+
+def summed_here(value, mesh_axis):
+    parts = lax.all_gather(value, mesh_axis)
+    return jnp.sum(parts, axis=0)
 
 
 def on_device(
@@ -50,7 +55,7 @@
     partial_sum = jnp.einsum(
         "ltc,lcd->td", context, joining_weight, preferred_element_type=jnp.float32
     )
-    summed = lax.psum(partial_sum.astype(jnp.bfloat16), "tensor").astype(jnp.float32)
+    summed = summed_here(partial_sum.astype(jnp.bfloat16), "tensor").astype(jnp.float32)
     joined_rows = lax.dynamic_slice_in_dim(summed, offset, own_rows, 0)
     token_pos = offset + jnp.arange(own_rows, dtype=jnp.int32)
     chain_of = token_pos // seq_len

time: 237 us -> 269 us (1.14)
  waiting for transfers between devices: 143 us -> 164 us
  other arithmetic: 12.2 us -> 23.6 us
    all_gather x0 -> x1, waiting for transfers between devices: none -> 108 us  [summed_here(): parts = lax.all_gather(value, mesh_axis)]
    psum x1 -> x0, waiting for transfers between devices: 86.9 us -> none  [on_device(): lax.psum(partial_sum.astype(jnp.bfloat16), 'tensor').astype(jnp.float32)]
    reduce_sum x0 -> x1, other arithmetic: none -> 12 us  [summed_here(): return jnp.sum(parts, axis=0)]
where the time goes in v1:
time: 269 us
  waiting for transfers between devices  164 us (61%)
  blocking collectives  39.8 us (15%)
  other arithmetic  23.6 us (9%)
  matrix products  19.5 us (7%)
  between operations  17.7 us (7%)
  local copies, waits for them, and re-layouts  4.04 us (2%)
    all_gather x1, waiting for transfers between devices, summed_here(): parts = lax.all_gather(value, mesh_axis)  108 us
    psum x1, blocking collectives, on_device(): lax.psum((local_gain, local_loss, jnp.sum(token_weight)), ('dp', 'tensor'))  39.8 us
    all_gather x1, waiting for transfers between devices, on_device(): lax.all_gather(grad_joined, 'tensor', axis=0, tiled=True)  34.6 us
    reduce_scatter x1, waiting for transfers between devices, on_device(): lax.psum_scatter(grad_total.astype(jnp.bfloat16), 'dp', scatter_dimension...  21.3 us
    reduce_sum x1, other arithmetic, summed_here(): return jnp.sum(parts, axis=0)  12 us
    sub x1, matrix products, on_device(): exponent = jnp.exp(scores - row_peak)  7.73 us
  transfers between devices with their start and end apart: 3, of which 3 were waited for; matrix products, arithmetic and copies ran while one was open for 1% of the time, Pallas kernels for 0%

profile of v1, /device:TPU:0, one launch (start us, length us, event | category | flops | bytes accessed | tf_op | source)
XLA Modules:
  0.0 268.7 jit_solution(17279010306690435108)
XLA Ops:
  7.2 0.0 all-gather.6.cloned.1.call-start
  8.0 0.4 fusion.4
  8.4 2.0 reshape.122
  10.4 1.0 reshape.123
  11.4 1.0 copy.17
  12.4 7.7 %fusion.39 = (f32[2,1024]{1,0:T(2,128)S(1)}, f32[2,1024,1024]{1,2,0:T(8,128)}) fusion(pred[1024,1024]{0,1:T(8,128)(4,1)S(1)} %fusion.4, bf16[1024,2,128]{2,1,0:T(2,128)(2,1)} %reshape.123, bf16[1024,2,128]{2,1,0:T(2,128)(2,1)} %reshape.122), kind=kOutput, calls=%fused_computation.54 | convolution fusion | flops 545260544 | bytes 10493952 | tf_op jit(solution)/shard_map/sub | solution.py:44
  20.2 4.1 %fusion.20 = bf16[2,1024,128]{1,2,0:T(8,128)(2,1)S(1)} fusion(bf16[1024,2,128]{0,2,1:T(8,128)(2,1)S(1)} %bitcast.25, f32[2,1024,1024]{1,2,0:T(8,128)} %get-tuple-element.13, f32[2,1024]{1,0:T(2,128)S(1)} %get-tuple-element.12), kind=kOutput, calls=%fused_computation.29 | convolution fusion | flops 541327360 | bytes 9445376 | tf_op jit(solution)/shard_map/lchqk,lckhd->lcqhd/dot_general | solution.py:46
  24.3 3.2 %convolution_convert_fusion = bf16[1024,2048]{1,0:T(8,128)(2,1)} fusion(bf16[1024,256]{0,1:T(8,128)(2,1)S(1)} %bitcast.23, bf16[1,256,2048]{2,1,0:T(8,128)(2,1)S(1)} %copy-done), kind=kOutput, calls=%fused_computation.11 | convolution fusion | flops 1075838976 | bytes 5767168 | tf_op jit(solution)/shard_map/ltc,lcd->td/dot_general | solution.py:55
  27.5 0.0 all-gather.6.cloned.1.call-update
  27.5 0.0 all-gather.4.cloned.1.call-start
  28.2 108.1 %all-gather.6.cloned.1.call-done = bf16[4096,2048]{1,0:T(8,128)(2,1)} async-done(((bf16[1024,2048]{1,0:T(8,128)(2,1)}), bf16[4096,2048]{1,0:T(8,128)(2,1)}) %all-gather.6.cloned.1.call-update) | async-done | bytes 16777232 | tf_op jit(solution)/shard_map/all_gather | solution.py:13
  136.3 12.0 %reduce_sum.76 = bf16[1024,2048]{1,0:T(8,128)(2,1)} reduce(bf16[4,1024,2048]{2,1,0:T(8,128)(2,1)} %bitcast.22, bf16[]{:T(256)} %constant.49.clone.1), dimensions={0}, to_apply=%region_2.3 | reduce | flops 6291456 | bytes 20971522 | tf_op jit(solution)/shard_map/reduce_sum | solution.py:14
  148.3 1.5 fusion.19
  149.9 2.3 fusion.18
  152.2 3.4 %fusion.17 = (bf16[256,2048]{1,0:T(8,128)(2,1)}, bf16[256,2048]{1,0:T(8,128)(2,1)}) fusion(bf16[256,2048]{1,0:T(8,128)(2,1)S(1)} %copy-done.1, f32[256]{0:T(256)S(1)} %broadcast_multiply_fusion.1, f32[256]{0:T(256)S(1)} %broadcast_multiply_fusion, f32[2048]{0:T(1024)S(1)} %copy-done.5, f32[256]{0:T(256)S(1)} %add_rsqrt_fusion, ...), kind=kLoop, calls=%fused_computation.25 | loop fusion | flops 6291456 | bytes 4205572 | tf_op jit(solution)/shard_map/convert_element_type | solution.py:78
  155.6 0.0 all-gather.4.cloned.1.call-update
  155.6 0.0 reduce-scatter.2.cloned.1.call-start
  155.7 34.6 %all-gather.4.cloned.1.call-done = bf16[1024,2048]{1,0:T(8,128)(2,1)} async-done(((bf16[256,2048]{1,0:T(8,128)(2,1)}), bf16[1024,2048]{1,0:T(8,128)(2,1)}) %all-gather.4.cloned.1.call-update) | async-done | bytes 4194320 | tf_op jit(solution)/shard_map/all_gather | solution.py:85
  190.3 4.4 %fusion.11 = bf16[1,256,2048]{2,1,0:T(8,128)(2,1)} fusion(bf16[1024,256]{0,1:T(8,128)(2,1)S(1)} %bitcast.24, bf16[1024,2048]{1,0:T(8,128)(2,1)} %all-gather.4.cloned.1.call-done), kind=kOutput, calls=%fused_computation.19 | convolution fusion | flops 1074266112 | bytes 5767168 | tf_op jit(solution)/shard_map/ltc,td->lcd/dot_general | solution.py:82
  194.7 0.7 multiply_reduce_fusion.1
  195.4 39.8 %all-reduce = (f32[]{:T(128)}, f32[2048]{0:T(1024)S(1)}, f32[]{:T(128)}) all-reduce(f32[]{:T(128)} %get-tuple-element.15, f32[2048]{0:T(1024)S(1)} %get-tuple-element.4, f32[]{:T(128)} %get-tuple-element.14), channel_id=1, replica_groups=mesh['dp'=8,'tensor'=4] {'dp','tensor'}, use_global_device_ids=true, to_apply=%region_7.8 | all-reduce | flops 2050 | bytes 16400 | tf_op jit(solution)/shard_map/psum | solution.py:79
  236.4 1.2 broadcast_divide_fusion
  237.6 21.3 %reduce-scatter.2.cloned.1.call-done = bf16[1,256,256]{2,1,0:T(8,128)(2,1)} async-done(((bf16[1,256,2048]{2,1,0:T(8,128)(2,1)}), bf16[1,256,256]{2,1,0:T(8,128)(2,1)}) %reduce-scatter.2.cloned.1.call-update) | async-done | bytes 131088 | tf_op jit(solution)/shard_map/reduce_scatter | solution.py:88
  258.9 2.1 divide_convert_fusion.4
  (17 shorter events, 0.1 us)
Async XLA Ops:
  7.2 17.1 %copy-start = (bf16[1,256,2048]{2,1,0:T(8,128)(2,1)S(1)}, bf16[1,256,2048]{2,1,0:T(8,128)(2,1)}, u32[]{:S(2)}) copy-start(bf16[1,256,2048]{2,1,0:T(8,128)(2,1)} %param.11) | copy-start | bytes 3145732
  7.2 3.3 %copy-start.2 = (bf16[1,1024,256]{2,1,0:T(8,128)(2,1)S(1)}, bf16[1,1024,256]{2,1,0:T(8,128)(2,1)}, u32[]{:S(2)}) copy-start(bf16[1,1024,256]{2,1,0:T(8,128)(2,1)} %param.9) | copy-start | bytes 1572868
  7.2 4.2 %copy-start.3 = (bf16[1,1024,256]{2,1,0:T(8,128)(2,1)S(1)}, bf16[1,1024,256]{2,1,0:T(8,128)(2,1)}, u32[]{:S(2)}) copy-start(bf16[1,1024,256]{2,1,0:T(8,128)(2,1)} %param.10) | copy-start | bytes 1572868
  7.2 129.1 %all-gather.6.cloned.1.call-start = ((), (), s32[]{:S(2)}) async-start(), calls=%async_computation.3 | async-start | bytes 20971520 | tf_op jit(solution)/shard_map/all_gather | solution.py:13
  12.4 7.7 %copy-start.4 = (bf16[1,1024,256]{1,2,0:T(8,128)(2,1)S(1)}, bf16[1,1024,256]{1,2,0:T(8,128)(2,1)}, u32[]{:S(2)}) copy-start(bf16[1,1024,256]{1,2,0:T(8,128)(2,1)} %copy.17) | copy-start | bytes 1572868
  27.5 162.7 %all-gather.4.cloned.1.call-start = ((), (), s32[]{:S(2)}) async-start(), calls=%async_computation.1 | async-start | bytes 5242880 | tf_op jit(solution)/shard_map/all_gather | solution.py:85
  136.3 13.5 %copy-start.1 = (bf16[256,2048]{1,0:T(8,128)(2,1)S(1)}, bf16[256,2048]{1,0:T(8,128)(2,1)}, u32[]{:S(2)}) copy-start(bf16[256,2048]{1,0:T(8,128)(2,1)} %param.13) | copy-start | bytes 3145732
  136.3 13.6 %copy-start.5 = (f32[2048]{0:T(1024)S(1)}, f32[2048]{0:T(1024)}, u32[]{:S(2)}) copy-start(f32[2048]{0:T(1024)} %param.12) | copy-start | bytes 24580
  155.6 103.2 %reduce-scatter.2.cloned.1.call-start = ((), (), s32[]{:S(2)}) async-start(), calls=%async_computation.2 | async-start | bytes 1179648 | tf_op jit(solution)/shard_map/reduce_scatter | solution.py:88
Sparse Core Ops, SparseCore 0:
  27.6 108.6 all-gather.5
  155.8 34.4 all-gather.3
  194.8 63.9 reduce-scatter.1
